TPU v7x, 32 devices: a whole 2x2x4 slice. The times are simulated.
32 devices in a mesh: blen: 4 (over z), tm: 8 (over y, x, core).
Axes of the slice: x: 2, y: 2, z: 4, core: 2. Of those that a mesh axis runs over, the one named last changes fastest.
Arguments:
- model_grid: bfloat16 [256, 2, 512, 512], P(('blen', 'tm')), may hold values from -6 to 6
- vis_values: float32 [2, 16384], P(None, ('blen', 'tm')), may hold values from -6 to 6
- weights: float32 [16384], P(('blen', 'tm')), may hold values from 0.3 to 3
- flags: int32 [16384], P(('blen', 'tm')), may hold values 0 or 1
- uv_frac: float32 [2, 16384], P(None, ('blen', 'tm')), may hold values from 0 to 1
- cell_offset: int32 [2, 16384], P(None, ('blen', 'tm')), may hold values from 3 to 507
- tile_index: int32 [16384, 1], P(('blen', 'tm')), may hold values from 0 to 255; in each aligned block of 512 rows (0 to 511, 512 to 1023, ...) at most 4 rows name the same one
Outputs:
- gradient: float32 [8192, 8192], P(('blen', 'tm'))
- weighted_residual: float32 [2, 16384], P(None, ('blen', 'tm'))
Inputs may be any that keep to these rules, and one draw needn't show every extreme that they name: `tile_index`: in the rows of one device no tile is named by more than 4 rows, and some device has a tile named by exactly 4 rows.
All inputs are finite; a program needn't handle non-finite values. No bound on the sum of `flags` on one device may be relied on, other than what follows from the above.
Results may differ from a plain program's by a relative error of at most 0.0095.
Values sent between devices are 32-bit elements; how exact they have to be, the bound alone decides.
No kernel may reach another device: no remote copies, remote signals or barrier semaphores. Data moves between devices by JAX's collectives and lax.ppermute only.
A program may use at most 192 MiB of HBM per device.

v0:
```python
import math
import jax
import jax.numpy as jnp
from jax import lax
from jax.sharding import PartitionSpec as P

NPIX = 8192
KSUP = 8
NT = 16
MOST = 4
kernel_scale = 0.5
highest = lax.Precision.HIGHEST


def taps_full(offsets, fractions, tile_side):
    cell_ids = lax.broadcasted_iota(jnp.int32, offsets.shape + (tile_side,), offsets.ndim)
    shifted = cell_ids - offsets[..., None]
    distance = shifted.astype(jnp.float32) - fractions[..., None]
    inside = (shifted >= 1 - KSUP // 2) & (shifted <= KSUP // 2)
    values = jnp.exp(-kernel_scale * distance * distance)
    return jnp.where(inside, values, 0.0).astype(jnp.bfloat16)


def phase_table(row_count, col_count, period):
    row_ids = lax.broadcasted_iota(jnp.int32, (row_count, col_count), 0)
    col_ids = lax.broadcasted_iota(jnp.int32, (row_count, col_count), 1)
    angles = 2.0 * math.pi / period * (row_ids * col_ids % period).astype(jnp.float32)
    return (jnp.cos(angles), jnp.sin(angles))


def complex_block(cos_part, sin_part):
    return jnp.stack([jnp.stack([cos_part, -sin_part]), jnp.stack([sin_part, cos_part])])


def on_device(model_grid, vis_values, weights, flags, uv_frac, cell_offset, tile_index):
    blen_size = lax.axis_size("blen")
    tm_size = lax.axis_size("tm")
    devices = blen_size * tm_size
    per_dev = model_grid.shape[0]
    tile_side = model_grid.shape[2]
    vis_count = weights.shape[0]
    ntiles = per_dev * devices
    total_slots = ntiles * MOST
    tile_ids = tile_index[:, 0]
    matches = tile_ids[:, None] == lax.broadcasted_iota(jnp.int32, (vis_count, ntiles), 1)
    counts = jnp.sum(matches.astype(jnp.int32), axis=0)
    starts = jnp.cumsum(counts) - counts
    sorting = jnp.argsort(tile_ids, stable=True)
    position = (
        jnp.zeros((vis_count,), jnp.int32).at[sorting].set(jnp.arange(vis_count, dtype=jnp.int32))
    )
    first_slot = jnp.sum(jnp.where(matches, starts[None, :], 0), axis=1)
    rank_in_tile = position - first_slot
    owner_dev = tile_ids // per_dev
    local_tile = tile_ids % per_dev
    slot_of = (local_tile * devices + owner_dev) * MOST + rank_in_tile
    weighted = weights * flags.astype(jnp.float32)
    float_fields = jnp.stack([vis_values[0], vis_values[1], weighted, uv_frac[0], uv_frac[1]])
    send_float = jnp.zeros((5, total_slots), jnp.float32).at[:, slot_of].set(float_fields)
    send_int = jnp.zeros((2, total_slots), jnp.int32).at[:, slot_of].set(cell_offset)
    recv_float, recv_int = (
        lax.all_to_all(
            send_float.reshape(5, per_dev, devices, MOST),
            ("blen", "tm"),
            split_axis=2,
            concat_axis=2,
            tiled=True,
        ),
        lax.all_to_all(
            send_int.reshape(2, per_dev, devices, MOST),
            ("blen", "tm"),
            split_axis=2,
            concat_axis=2,
            tiled=True,
        ),
    )
    owner_rows = devices * MOST
    block_rows = 512 if owner_rows % 512 == 0 else owner_rows
    block_count = owner_rows // block_rows
    float_blocks = recv_float.reshape(5, per_dev, block_count, block_rows).transpose(2, 0, 1, 3)
    int_blocks = recv_int.reshape(2, per_dev, block_count, block_rows).transpose(2, 0, 1, 3)

    def grid_step(adjoint, inputs):
        part_float, part_int = inputs
        taps_u = taps_full(part_int[0], part_float[3], tile_side)
        taps_v = taps_full(part_int[1], part_float[4], tile_side)
        partial_sums = jnp.einsum(
            "qrj,qcji->qrci", taps_v, model_grid, preferred_element_type=jnp.float32
        )
        predicted = jnp.sum(partial_sums * taps_u[:, :, None, :], axis=-1)
        observed = jnp.stack([part_float[0], part_float[1]], axis=-1)
        residual = part_float[2][..., None] * (predicted - observed)
        spread = (residual[..., None] * taps_u[:, :, None, :]).astype(jnp.bfloat16)
        adjoint = adjoint + jnp.einsum(
            "qrj,qrci->qcji", taps_v, spread, preferred_element_type=jnp.float32
        )
        return (adjoint, jnp.moveaxis(residual, -1, 0))

    start_adjoint = jnp.zeros((per_dev, 2, tile_side, tile_side), jnp.float32)
    adjoint, residual_blocks = lax.scan(grid_step, start_adjoint, (float_blocks, int_blocks))
    residual_slots = residual_blocks.transpose(1, 2, 0, 3).reshape(2, per_dev, owner_rows)
    returned = lax.all_to_all(
        residual_slots.reshape(2, per_dev, devices, MOST),
        ("blen", "tm"),
        split_axis=2,
        concat_axis=2,
        tiled=True,
    )
    weighted_residual = returned.reshape(2, total_slots)[:, slot_of]
    relaid = lax.all_to_all(adjoint, "tm", split_axis=2, concat_axis=0, tiled=True)
    tile_cols = NT // blen_size
    col_slice = tile_side // tm_size
    pieces = relaid.reshape(NT, tile_cols, 2, col_slice, tile_side)
    cos_small, sin_small = phase_table(NT, NT, NT)
    small_turn = complex_block(cos_small, sin_small)
    cos_twist, sin_twist = phase_table(NT, tile_side, NPIX)
    cos_tile, sin_tile = phase_table(tile_side, tile_side, tile_side)
    tile_turn = complex_block(cos_tile, sin_tile)
    section_one = jnp.einsum("acnt,tvcji->anvji", small_turn, pieces, precision=highest)
    twist_c = cos_twist[:, None, None, :]
    twist_s = sin_twist[:, None, None, :]
    turned = jnp.stack(
        [
            section_one[0] * twist_c - section_one[1] * twist_s,
            section_one[0] * twist_s + section_one[1] * twist_c,
        ]
    )
    columns = jnp.einsum("acmi,cnvji->amnvj", tile_turn, turned, precision=highest)
    rows_dev = NPIX // devices
    spread_cols = rows_dev * tile_cols * col_slice
    packed = columns.reshape(2, 1, devices, spread_cols)
    landed = lax.all_to_all(packed, ("blen", "tm"), split_axis=2, concat_axis=1, tiled=True)
    landed = landed.reshape(2, blen_size, tm_size, rows_dev, tile_cols, col_slice)
    small_split = small_turn.reshape(2, 2, NT, blen_size, tile_cols)
    section_two = jnp.einsum("acnpv,cptrvj->antrj", small_split, landed, precision=highest)
    twist_cv = cos_twist.reshape(NT, tm_size, 1, col_slice)
    twist_sv = sin_twist.reshape(NT, tm_size, 1, col_slice)
    turned_rows = jnp.stack(
        [
            section_two[0] * twist_cv - section_two[1] * twist_sv,
            section_two[0] * twist_sv + section_two[1] * twist_cv,
        ]
    )
    real_turn = jnp.stack([cos_tile, -sin_tile]).reshape(2, tile_side, tm_size, col_slice)
    image_rows = jnp.einsum("cmtj,cntrj->rmn", real_turn, turned_rows, precision=highest)
    gradient = image_rows.reshape(rows_dev, NPIX) / NPIX
    return (gradient, weighted_residual)


def solution(mesh):
    in_specs = (
        P(("blen", "tm"), None, None, None),
        P(None, ("blen", "tm")),
        P(("blen", "tm")),
        P(("blen", "tm")),
        P(None, ("blen", "tm")),
        P(None, ("blen", "tm")),
        P(("blen", "tm"), None),
    )
    out_specs = (P(("blen", "tm"), None), P(None, ("blen", "tm")))
    return jax.shard_map(
        on_device, mesh=mesh, in_specs=in_specs, out_specs=out_specs, check_vma=False
    )
```

profile of v0, /device:TPU:0, one launch (start us, length us, event | category | flops | bytes accessed | tf_op | source)
XLA Modules:
  0.0 1047.1 jit_solution(14593329809357333968)
XLA Ops:
  3.0 4.4 sort.17
  14.8 7.3 all-to-all-start.1
  27.3 3.0 all-to-all-done.1
  30.3 2.8 all-to-all-start
  33.3 7.1 all-to-all-done
  43.2 5.3 multiply_reduce_fusion
  48.5 7.2 convolution_bitcast_fusion
  55.7 25.1 %copy.78 = f32[8,2,512,512]{3,1,0,2:T(2,128)} copy(f32[8,2,512,512]{2,3,1,0:T(8,128)} %convolution_bitcast_fusion) | data formatting | bytes 33554432 | tf_op jit(solution)/shard_map/while/body/eval_jaxpr/qrj,qrci->qcji/transpose | solution.py:94
  80.8 6.0 all-to-all-start.2
  87.2 3.9 fusion.60
  91.0 4.1 fusion.58
  97.8 173.0 %all-to-all-done.2 = f32[8,2,512,512]{3,1,0,2:T(2,128)} async-done(((f32[8,2,512,512]{3,1,0,2:T(2,128)}), f32[8,2,512,512]{3,1,0,2:T(2,128)}, u32[]{:S(2)}, u32[]{:S(2)}) %all-to-all-start.2) | async-done | bytes 16777248 | tf_op jit(solution)/shard_map/all_to_all | solution.py:110
  270.8 2.6 all-to-all-start.4
  273.4 11.0 %copy.79 = f32[8,2,512,512]{3,2,1,0:T(8,128)S(1)} copy(f32[8,2,512,512]{3,1,0,2:T(2,128)} %all-to-all-done.2) | data formatting | bytes 33554432 | tf_op jit(solution)/shard_map/all_to_all | solution.py:110
  284.4 6.7 copy.80
  291.1 42.0 %fusion.11 = f32[2,16,4,64,512]{4,1,3,2,0:T(8,128)} fusion(f32[16,4,2,64,512]{4,3,2,1,0:T(8,128)} %bitcast.109, f32[1,2,16,16]{3,2,1,0:T(8,128)S(1)} %get-tuple-element.44, f32[1,2,16,16]{3,2,1,0:T(8,128)S(1)} %get-tuple-element.43), kind=kOutput, calls=%fused_computation.23 | convolution fusion | flops 1610613760 | bytes 33558528 | tf_op jit(solution)/shard_map/acnt,tvcji->anvji/dot_general | solution.py:119
  333.1 7.1 multiply_subtract_fusion.1
  340.2 6.4 pad_maximum_fusion
  346.6 67.2 %fusion.14 = f32[2,512,16,4,64]{1,4,3,2,0:T(8,128)} fusion(f32[2,16,4,64,512]{4,1,3,2,0:T(8,128)} %pad_maximum_fusion, f32[1,2,512,512]{3,2,1,0:T(8,128)S(1)} %copy-done, f32[1,2,512,512]{3,2,1,0:T(8,128)S(1)} %get-tuple-element.34), kind=kOutput, calls=%fused_computation.24 | convolution fusion | flops 51540656128 | bytes 37748736 | tf_op jit(solution)/shard_map/acmi,cnvji->amnvj/dot_general | solution.py:128
  413.8 31.1 %copy.83 = f32[2,512,16,4,64]{4,3,2,1,0:T(4,128)} copy(f32[2,512,16,4,64]{1,4,3,2,0:T(8,128)} %fusion.14) | data formatting | bytes 33554432 | tf_op jit(solution)/shard_map/acmi,cnvji->amnvj/dot_general | solution.py:128
  444.9 27.4 %reshape.436 = f32[2,1,32,65536]{3,2,0,1:T(8,128)} reshape(f32[2,512,16,4,64]{4,3,2,1,0:T(4,128)} %copy.83) | data formatting | bytes 33554432 | tf_op jit(solution)/shard_map/reshape | solution.py:131
  472.2 28.6 %copy.84 = f32[2,1,32,65536]{3,0,1,2:T(2,128)} copy(f32[2,1,32,65536]{3,2,0,1:T(8,128)} %reshape.436) | data formatting | bytes 33554432 | tf_op jit(solution)/shard_map/reshape | solution.py:131
  500.9 6.0 all-to-all-start.3
  507.1 4.2 sine_negate_fusion
  516.5 363.0 %all-to-all-done.3 = f32[2,1,32,65536]{3,0,1,2:T(2,128)} async-done(((f32[2,1,32,65536]{3,0,1,2:T(2,128)}), f32[2,1,32,65536]{3,0,1,2:T(2,128)}, u32[]{:S(2)}, u32[]{:S(2)}) %all-to-all-start.3) | async-done | bytes 16777248 | tf_op jit(solution)/shard_map/all_to_all | solution.py:132
  879.5 38.4 %reshape.487 = f32[2,4,8,256,4,64]{5,4,3,0,2,1:T(4,128)} reshape(f32[2,1,32,65536]{3,0,1,2:T(2,128)} %all-to-all-done.3) | data formatting | bytes 33554432 | tf_op jit(solution)/shard_map/reshape | solution.py:133
  918.0 30.9 %copy.86 = f32[2,4,8,256,4,64]{3,4,1,0,5,2:T(4,128)} copy(f32[2,4,8,256,4,64]{5,4,3,0,2,1:T(4,128)} %reshape.487) | data formatting | bytes 33554432 | tf_op jit(solution)/shard_map/reshape | solution.py:133
  948.8 31.8 %fusion.17 = f32[2,16,8,256,64]{3,1,4,2,0:T(8,128)S(1)} fusion(f32[2,4,8,256,4,64]{3,4,1,0,5,2:T(4,128)} %copy.86, f32[2,2,16,4,4,1,1]{2,4,3,1,6,5,0:T(4,128)S(1)} %maximum_bitcast_fusion.17), kind=kOutput, calls=%fused_computation.25 | convolution fusion | flops 1610612736 | bytes 33558528 | tf_op jit(solution)/shard_map/acnpv,cptrvj->antrj/dot_general | solution.py:135
  980.6 2.8 multiply_subtract_fusion
  985.2 42.3 %fusion.10 = f32[256,512,16]{1,0,2:T(8,128)} fusion(f32[2,16,8,256,64]{3,1,4,2,0:T(8,128)S(1)} %pad_maximum_fusion.1, f32[1,512,8,64]{1,3,2,0:T(8,128)S(1)} %get-tuple-element.56, f32[1,512,8,64]{1,3,2,0:T(8,128)S(1)} %get-tuple-element.57), kind=kOutput, calls=%fused_computation.18 | convolution fusion | flops 25772425216 | bytes 27262976 | tf_op jit(solution)/shard_map/cmtj,cntrj->rmn/dot_general | solution.py:145
  1027.6 10.3 copy.88
  1037.9 8.9 copy.92
  (60 shorter events, 28.0 us)
Async XLA Ops:
  11.4 14.1 %copy-start.1 = (s32[512]{0:T(512)}, s32[512]{0:T(512)S(1)}, u32[]{:S(2)}) copy-start(s32[512]{0:T(512)S(1)} %compare_select_fusion) | copy-start | bytes 6148
  14.8 15.5 %all-to-all-start.1 = ((s32[2,8,32,4]{1,3,0,2:T(4,128)}), s32[2,8,32,4]{1,3,0,2:T(4,128)S(1)}, u32[]{:S(2)}, u32[]{:S(2)}) async-start(s32[2,8,32,4]{1,3,0,2:T(4,128)} %copy.70), calls=%async_computation.1 | async-start | bytes 262144 | tf_op jit(solution)/shard_map/all_to_all | solution.py:69
  30.3 10.1 all-to-all-start
  80.8 190.0 %all-to-all-start.2 = ((f32[8,2,512,512]{3,1,0,2:T(2,128)}), f32[8,2,512,512]{3,1,0,2:T(2,128)}, u32[]{:S(2)}, u32[]{:S(2)}) async-start(f32[8,2,512,512]{3,1,0,2:T(2,128)} %copy.78), calls=%async_computation.2 | async-start | bytes 33554432 | tf_op jit(solution)/shard_map/all_to_all | solution.py:110
  270.8 230.0 %all-to-all-start.4 = ((f32[2,8,32,4]{1,3,0,2:T(4,128)}), f32[2,8,32,4]{1,3,0,2:T(4,128)S(1)}, u32[]{:S(2)}, u32[]{:S(2)}) async-start(f32[2,8,32,4]{1,3,0,2:T(4,128)} %copy.90), calls=%async_computation.4 | async-start | bytes 262144 | tf_op jit(solution)/shard_map/all_to_all | solution.py:102
  340.2 6.4 copy-start
  500.9 6.0 copy-start.2
  500.9 378.7 %all-to-all-start.3 = ((f32[2,1,32,65536]{3,0,1,2:T(2,128)}), f32[2,1,32,65536]{3,0,1,2:T(2,128)}, u32[]{:S(2)}, u32[]{:S(2)}) async-start(f32[2,1,32,65536]{3,0,1,2:T(2,128)} %copy.84), calls=%async_computation.3 | async-start | bytes 33554432 | tf_op jit(solution)/shard_map/all_to_all | solution.py:132
where the time goes:
time: 1060 us; the launch traced here: 1050 us
  waiting for transfers between devices  546 us (52%)
  local copies, waits for them, and re-layouts  235 us (22%)
  matrix products  196 us (18%)
  other arithmetic  44 us (4%)
  starting transfers between devices  24.7 us (2%)
    all_to_all x1, waiting for transfers between devices, on_device(): lax.all_to_all(packed, ('blen', 'tm'), split_axis=2, concat_axis=1, tiled...  363 us
    all_to_all x1, waiting for transfers between devices, on_device(): lax.all_to_all(adjoint, 'tm', split_axis=2, concat_axis=0, tiled=True)  173 us
    reshape x2, local copies, waits for them, and re-layouts, on_device(): landed.reshape(2, blen_size, tm_size, rows_dev, tile_cols, col_slice)  69.3 us
    dot_general x1, matrix products, on_device(): jnp.einsum('acmi,cnvji->amnvj', tile_turn, turned, precision=highest)  67.2 us
    reshape x2, local copies, waits for them, and re-layouts, on_device(): packed = columns.reshape(2, 1, devices, spread_cols)  56 us
    dot_general x1, matrix products, on_device(): jnp.einsum('cmtj,cntrj->rmn', real_turn, turned_rows, precision=highest)  42.3 us
    dot_general x1, matrix products, on_device(): jnp.einsum('acnt,tvcji->anvji', small_turn, pieces, precision=highest)  42 us
    dot_general x1, matrix products, on_device(): jnp.einsum('acnpv,cptrvj->antrj', small_split, landed, precision=highest)  31.8 us
  transfers between devices with their start and end apart: 5, of which 4 were waited for; matrix products, arithmetic and copies ran while one was open for 24% of the time, Pallas kernels for 0%

commit v1 on v0

--- a/solution.py
+++ b/solution.py
@@ -129,7 +129,15 @@
     rows_dev = NPIX // devices
     spread_cols = rows_dev * tile_cols * col_slice
     packed = columns.reshape(2, 1, devices, spread_cols)
-    landed = lax.all_to_all(packed, ("blen", "tm"), split_axis=2, concat_axis=1, tiled=True)
+    landed = jnp.concatenate(
+        lax.all_to_all(
+            jnp.stack(jnp.split(packed, lax.axis_size(("blen", "tm")), axis=2)),
+            ("blen", "tm"),
+            0,
+            0,
+        ),
+        axis=1,
+    )
     landed = landed.reshape(2, blen_size, tm_size, rows_dev, tile_cols, col_slice)
     small_split = small_turn.reshape(2, 2, NT, blen_size, tile_cols)
     section_two = jnp.einsum("acnpv,cptrvj->antrj", small_split, landed, precision=highest)

time: 1060 us -> 1160 us (1.094)
  local copies, waits for them, and re-layouts: 235 us -> 345 us
    unnamed x11 -> x44, local copies, waits for them, and re-layouts: 12.5 us -> 87 us
    another operation x2 -> x5, local copies, waits for them, and re-layouts: 0.19 us -> 70.7 us  [the longest x2 69.3 us: on_device(): landed.reshape(2, blen_size, tm_size, rows_dev, tile_cols, col_slice)]
    reshape x2 -> x1, local copies, waits for them, and re-layouts: 56 us -> 27.4 us  [on_device(): packed = columns.reshape(2, 1, devices, spread_cols)]
    reshape x2 -> x1, local copies, waits for them, and re-layouts: 69.3 us -> 62.3 us  [on_device(): jnp.concatenate(lax.all_to_all(jnp.stack(jnp.split(packed, lax.axis_size(...]
  transfers between devices with their start and end apart: 5 -> 5, of which waited for: 4 -> 4; matrix products, arithmetic and copies ran while one was open for 24% -> 25% of each run, Pallas kernels for 0% -> 0%
where the time goes in v1:
time: 1160 us; the launch traced here: 1150 us
  waiting for transfers between devices  546 us (47%)
  local copies, waits for them, and re-layouts  345 us (30%)
  matrix products  187 us (16%)
  other arithmetic  44 us (4%)
  starting transfers between devices  24.6 us (2%)
    all_to_all x1, waiting for transfers between devices, on_device(): lax.all_to_all(jnp.stack(jnp.split(packed, lax.axis_size(('blen', 'tm')),...  363 us
    all_to_all x1, waiting for transfers between devices, on_device(): lax.all_to_all(adjoint, 'tm', split_axis=2, concat_axis=0, tiled=True)  173 us
    unnamed x44, local copies, waits for them, and re-layouts  87 us
    another operation x2, local copies, waits for them, and re-layouts, on_device(): landed.reshape(2, blen_size, tm_size, rows_dev, tile_cols, col_slice)  69.3 us
    dot_general x1, matrix products, on_device(): jnp.einsum('acmi,cnvji->amnvj', tile_turn, turned, precision=highest)  67.2 us
    reshape x1, local copies, waits for them, and re-layouts, on_device(): jnp.concatenate(lax.all_to_all(jnp.stack(jnp.split(packed, lax.axis_size(...  62.3 us
    dot_general x1, matrix products, on_device(): jnp.einsum('cmtj,cntrj->rmn', real_turn, turned_rows, precision=highest)  42.3 us
    dot_general x1, matrix products, on_device(): jnp.einsum('acnt,tvcji->anvji', small_turn, pieces, precision=highest)  33.2 us
  transfers between devices with their start and end apart: 5, of which 4 were waited for; matrix products, arithmetic and copies ran while one was open for 25% of the time, Pallas kernels for 0%

profile of v1, /device:TPU:0, one launch (start us, length us, event | category | flops | bytes accessed | tf_op | source)
XLA Modules:
  0.0 1147.7 jit_solution(14902994199805064292)
XLA Ops:
  3.0 4.4 sort.17
  14.8 7.3 all-to-all-start.1
  33.3 7.1 all-to-all-done
  43.2 5.3 multiply_reduce_fusion
  48.5 7.2 convolution_bitcast_fusion
  55.7 25.1 %copy.140 = f32[8,2,512,512]{3,1,0,2:T(2,128)} copy(f32[8,2,512,512]{2,3,1,0:T(8,128)} %convolution_bitcast_fusion) | data formatting | bytes 33554432 | tf_op jit(solution)/shard_map/while/body/eval_jaxpr/qrj,qrci->qcji/transpose | solution.py:94
  80.8 5.9 all-to-all-start.2
  87.1 3.9 fusion.92
  90.9 4.1 fusion.90
  97.7 173.0 %all-to-all-done.2 = f32[8,2,512,512]{3,1,0,2:T(2,128)} async-done(((f32[8,2,512,512]{3,1,0,2:T(2,128)}), f32[8,2,512,512]{3,1,0,2:T(2,128)}, u32[]{:S(2)}, u32[]{:S(2)}) %all-to-all-start.2) | async-done | bytes 16777248 | tf_op jit(solution)/shard_map/all_to_all | solution.py:110
  273.3 11.0 copy.141
  284.3 6.7 copy.142
  291.0 33.2 %fusion.11 = f32[2,16,4,64,512]{4,1,3,2,0:T(8,128)} fusion(f32[16,4,2,64,512]{4,3,2,1,0:T(8,128)} %bitcast.301, f32[1,2,16,16]{3,2,1,0:T(8,128)S(1)} %get-tuple-element.44, f32[1,2,16,16]{3,2,1,0:T(8,128)S(1)} %get-tuple-element.43), kind=kOutput, calls=%fused_computation.24 | convolution fusion | flops 1610613760 | bytes 33558528 | tf_op jit(solution)/shard_map/acnt,tvcji->anvji/dot_general | solution.py:119
  324.2 7.1 multiply_subtract_fusion.1
  331.3 6.4 pad_maximum_fusion
  337.7 67.2 %fusion.14 = f32[2,512,16,4,64]{1,4,3,2,0:T(8,128)} fusion(f32[2,16,4,64,512]{4,1,3,2,0:T(8,128)} %pad_maximum_fusion, f32[1,2,512,512]{3,2,1,0:T(8,128)S(1)} %copy-done.1, f32[1,2,512,512]{3,2,1,0:T(8,128)S(1)} %get-tuple-element.34), kind=kOutput, calls=%fused_computation.25 | convolution fusion | flops 51540656128 | bytes 37748736 | tf_op jit(solution)/shard_map/acmi,cnvji->amnvj/dot_general | solution.py:128
  404.9 31.1 %copy.145 = f32[2,512,16,4,64]{4,3,2,1,0:T(4,128)} copy(f32[2,512,16,4,64]{1,4,3,2,0:T(8,128)} %fusion.14) | data formatting | bytes 33554432 | tf_op jit(solution)/shard_map/acmi,cnvji->amnvj/dot_general | solution.py:128
  436.0 27.4 %reshape.432 = f32[2,1,32,65536]{3,2,0,1:T(8,128)} reshape(f32[2,512,16,4,64]{4,3,2,1,0:T(4,128)} %copy.145) | data formatting | bytes 33554432 | tf_op jit(solution)/shard_map/reshape | solution.py:131
  466.8 4.2 fusion.88
  471.0 3.5 fusion.87
  474.5 3.5 fusion.86
  508.8 3.5 fusion.76
  539.1 6.0 all-to-all-start.3
  545.3 4.2 sine_negate_fusion
  554.7 363.0 %all-to-all-done.3 = f32[32,2,1,1,65536]{4,3,2,1,0:T(1,128)} async-done(((f32[32,2,1,1,65536]{4,3,2,1,0:T(1,128)}), f32[32,2,1,1,65536]{4,3,2,1,0:T(1,128)}, u32[]{:S(2)}, u32[]{:S(2)}) %all-to-all-start.3) | async-done | bytes 16777248 | tf_op jit(solution)/shard_map/all_to_all | solution.py:133
  917.8 62.3 %bitcast_reduce_fusion = f32[2,32,65536]{2,0,1:T(2,128)} fusion(f32[32,2,1,1,65536]{4,3,2,1,0:T(1,128)} %all-to-all-done.3), kind=kLoop, calls=%fused_computation.8 | loop fusion | bytes 33554432 | tf_op jit(solution)/shard_map/reshape | solution.py:132
  980.1 38.4 %reshape.483 = f32[2,4,8,256,4,64]{5,4,3,0,2,1:T(4,128)} reshape(f32[2,32,65536]{2,0,1:T(2,128)} %bitcast_reduce_fusion) | data formatting | bytes 33554432 | tf_op jit(solution)/shard_map/reshape;reshape | solution.py:141
  1018.5 30.9 %copy.178 = f32[2,4,8,256,4,64]{3,4,1,0,5,2:T(4,128)} copy(f32[2,4,8,256,4,64]{5,4,3,0,2,1:T(4,128)} %reshape.483) | data formatting | bytes 33554432 | tf_op jit(solution)/shard_map/reshape;reshape | solution.py:141
  1049.4 32.0 %fusion.17 = f32[2,16,8,256,64]{3,1,4,2,0:T(8,128)S(1)} fusion(f32[2,4,8,256,4,64]{3,4,1,0,5,2:T(4,128)} %copy.178, f32[2,2,16,4,4,1,1]{2,4,3,1,6,5,0:T(4,128)S(1)} %maximum_bitcast_fusion.17), kind=kOutput, calls=%fused_computation.26 | convolution fusion | flops 1610612736 | bytes 33558528 | tf_op jit(solution)/shard_map/acnpv,cptrvj->antrj/dot_general | solution.py:143
  1086.1 42.3 %fusion.10 = f32[256,512,16]{1,0,2:T(8,128)} fusion(f32[2,16,8,256,64]{3,1,4,2,0:T(8,128)S(1)} %pad_maximum_fusion.1, f32[1,512,8,64]{1,3,2,0:T(8,128)S(1)} %get-tuple-element.56, f32[1,512,8,64]{1,3,2,0:T(8,128)S(1)} %get-tuple-element.57), kind=kOutput, calls=%fused_computation.19 | convolution fusion | flops 25772425216 | bytes 27262976 | tf_op jit(solution)/shard_map/cmtj,cntrj->rmn/dot_general | solution.py:153
  1128.4 10.3 copy.180
  1138.6 8.9 copy.184
  (94 shorter events, 100.3 us)
Async XLA Ops:
  11.4 14.1 %copy-start.2 = (s32[512]{0:T(512)}, s32[512]{0:T(512)S(1)}, u32[]{:S(2)}) copy-start(s32[512]{0:T(512)S(1)} %compare_select_fusion) | copy-start | bytes 6148
  14.8 15.5 %all-to-all-start.1 = ((s32[2,8,32,4]{1,3,0,2:T(4,128)}), s32[2,8,32,4]{1,3,0,2:T(4,128)S(1)}, u32[]{:S(2)}, u32[]{:S(2)}) async-start(s32[2,8,32,4]{1,3,0,2:T(4,128)} %copy.132), calls=%async_computation.1 | async-start | bytes 262144 | tf_op jit(solution)/shard_map/all_to_all | solution.py:69
  30.3 10.1 all-to-all-start
  80.8 189.9 %all-to-all-start.2 = ((f32[8,2,512,512]{3,1,0,2:T(2,128)}), f32[8,2,512,512]{3,1,0,2:T(2,128)}, u32[]{:S(2)}, u32[]{:S(2)}) async-start(f32[8,2,512,512]{3,1,0,2:T(2,128)} %copy.140), calls=%async_computation.2 | async-start | bytes 33554432 | tf_op jit(solution)/shard_map/all_to_all | solution.py:110
  270.7 268.4 %all-to-all-start.4 = ((f32[2,8,32,4]{1,3,0,2:T(4,128)}), f32[2,8,32,4]{1,3,0,2:T(4,128)S(1)}, u32[]{:S(2)}, u32[]{:S(2)}) async-start(f32[2,8,32,4]{1,3,0,2:T(4,128)} %copy.182), calls=%async_computation.4 | async-start | bytes 262144 | tf_op jit(solution)/shard_map/all_to_all | solution.py:102
  331.3 6.4 copy-start.1
  463.4 55.7 %copy-start = (f32[2,1,32,65536]{3,2,0,1:T(8,128)S(1)}, f32[2,1,32,65536]{3,2,0,1:T(8,128)}, u32[]{:S(2)}) copy-start(f32[2,1,32,65536]{3,2,0,1:T(8,128)} %reshape.432) | copy-start | bytes 50331652
  539.1 6.0 copy-start.3
  539.1 378.7 %all-to-all-start.3 = ((f32[32,2,1,1,65536]{4,3,2,1,0:T(1,128)}), f32[32,2,1,1,65536]{4,3,2,1,0:T(1,128)}, u32[]{:S(2)}, u32[]{:S(2)}) async-start(f32[32,2,1,1,65536]{4,3,2,1,0:T(1,128)} %fusion.58), calls=%async_computation.3 | async-start | bytes 33554432 | tf_op jit(solution)/shard_map/all_to_all | solution.py:133
